TPU v7x, 32 devices: a whole 2x2x4 slice. The times are simulated.
32 devices in a mesh: group: 4 (over y, x), brick: 8 (over z, core).
Axes of the slice: x: 2, y: 2, z: 4, core: 2. Of those that a mesh axis runs over, the one named last changes fastest.
Arguments:
- populations: float32 [19, 8, 64, 128], P(None, 'group', 'brick'), may hold values from 0 to 1, as said below
- positions: float32 [3, 64, 642], P(None, ('group', 'brick')), may hold values from -6 to 6
- rest_shape: float32 [3, 642], replicated, may hold values from -6 to 6
- inverse: float32 [642, 642], replicated, may hold values from -2 to 2, as said below
- sample_cells: int32 [32, 64], P(('group', 'brick')), may hold values from 0 to 2047
- vertex_slots: int32 [32, 1284], P(('group', 'brick')), may hold values from 0 to 63, as said below
- pair_own: int32 [32, 2048], P(('group', 'brick')), may hold values from 0 to 1283
- pair_far: int32 [32, 2048], P(('group', 'brick')), may hold values from 0 to 1283
Outputs:
- new_populations: float32 [19, 8, 64, 128], P(None, 'group', 'brick')
- new_positions: float32 [3, 64, 642], P(None, ('group', 'brick'))
Inputs may be any that keep to these rules, and one draw needn't show every extreme that they name: Every population is positive and a cell's populations sum to between 0.6 and 1.4. inverse is symmetric. `vertex_slots`: on every device each slot 0 to 63 is named by at least one vertex.
All inputs are finite; a program needn't handle non-finite values.
Results may differ from a plain program's by a relative error of at most 0.0001.
Values sent between devices are 32-bit elements; how exact they have to be, the bound alone decides.
A program may use at most 64 MiB of HBM per device.

v0:
```python
import functools

import jax
import jax.numpy as jnp
from jax import lax
from jax.experimental import pallas as pl
from jax.experimental.pallas import tpu as pltpu
from jax.sharding import PartitionSpec as P

ITERS = 4
STEPS = 2


velocities = [
    (0, 0, 0),
    (0, 0, 1),
    (0, 0, -1),
    (1, 0, 0),
    (-1, 0, 0),
    (0, 1, 0),
    (0, -1, 0),
    (1, 1, 0),
    (-1, -1, 0),
    (1, -1, 0),
    (-1, 1, 0),
    (1, 0, 1),
    (-1, 0, -1),
    (1, 0, -1),
    (-1, 0, 1),
    (0, 1, 1),
    (0, -1, -1),
    (0, 1, -1),
    (0, -1, 1),
]
weights_table = [1.0 / 3.0] + [1.0 / 18.0] * 6 + [1.0 / 36.0] * 12
relax_time = 0.8
contact_gain = 0.5
contact_range = 6.0
coupling_gain = 0.05
mass_weight = 1.0
shape_weight = 1.0
time_step = 1.0


def extended(cells, sides, width):
    for axis, dim in sides:
        count = lax.axis_size(axis)
        head = lax.slice_in_dim(cells, 0, width, axis=dim)
        tail = lax.slice_in_dim(cells, cells.shape[dim] - width, cells.shape[dim], axis=dim)
        cells = jnp.concatenate(
            [
                lax.ppermute(tail, axis, [(i, (i + 1) % count) for i in range(count)]),
                cells,
                lax.ppermute(head, axis, [((i + 1) % count, i) for i in range(count)]),
            ],
            axis=dim,
        )
    return cells


def shifted_2(array, axis, by):
    peers = lax.axis_size(axis)
    return lax.ppermute(array, axis, [(i, (i + by) % peers) for i in range(peers)])


def moments(populations):
    table = jnp.array(velocities, jnp.float32)
    density = jnp.sum(populations, axis=0)
    momentum = jnp.einsum("iq,ixyz->qxyz", table, populations, precision=lax.Precision.HIGHEST)
    return (density, momentum)


def collide(populations, force):
    table = jnp.array(velocities, jnp.float32)
    weight_col = jnp.array(weights_table, jnp.float32)[:, None, None, None]
    density, momentum = moments(populations)
    veloc = (momentum + 0.5 * force) / density
    project = jnp.einsum("iq,qxyz->ixyz", table, veloc, precision=lax.Precision.HIGHEST)
    forcing = jnp.einsum("iq,qxyz->ixyz", table, force, precision=lax.Precision.HIGHEST)
    square = jnp.sum(veloc * veloc, axis=0)
    equil = weight_col * density * (1.0 + 3.0 * project + 4.5 * project * project - 1.5 * square)
    return populations - (populations - equil) / relax_time + 3.0 * weight_col * forcing


def shifted(padded, index, width_x, width_y):
    step_x, step_y, step_z = velocities[index]
    piece = padded[1 - step_x : 1 - step_x + width_x, 1 - step_y : 1 - step_y + width_y, :]
    return jnp.roll(piece, step_z, axis=2)


def stream(post):
    width_x, width_y = (post.shape[1], post.shape[2])
    padded = extended(post, (("group", 1), ("brick", 2)), 1)
    moved = [shifted(padded[index], index, width_x, width_y) for index in range(19)]
    return jnp.stack(moved, axis=0)


LANES = 128
BODY_ROWS = 4


def pieces(value):
    high = value.astype(jnp.bfloat16)
    rest = value - high.astype(jnp.float32)
    middle = rest.astype(jnp.bfloat16)
    low = (rest - middle.astype(jnp.float32)).astype(jnp.bfloat16)
    return high, middle, low


def pick(points, hot, block, body):
    rows, width = points.shape
    blocks = width // LANES
    table = jnp.concatenate([points[:, h * LANES : (h + 1) * LANES] for h in range(blocks)], axis=0)
    got = jnp.dot(jnp.concatenate(pieces(table), axis=0), hot, preferred_element_type=jnp.float32)
    size = rows * blocks
    got = got[:size] + got[size : 2 * size] + got[2 * size :]
    total = jnp.zeros((rows, hot.shape[1]), jnp.float32)
    for h in range(blocks):
        total = total + jnp.where(block == h, got[h * rows : (h + 1) * rows], 0.0)
    row_body = lax.broadcasted_iota(jnp.int32, total.shape, 0) // BODY_ROWS
    total = jnp.where(row_body == body, total, 0.0)
    out = total
    for k in range(1, rows // BODY_ROWS):
        out = out + pltpu.roll(total, k * BODY_ROWS, 0)
    return out


def bodies_kernel(
    count, verts, shape_ref, predicted_ref, rest_ref, high_ref, middle_ref, index_ref, out_ref,
    own_hot, far_hot, current, lower, send_sem, recv_sem,
):
    me = lax.axis_index("brick")
    group = lax.axis_index("group")
    above = lax.rem(me + 1, count)
    below = lax.rem(me + count - 1, count)
    barrier = pltpu.get_barrier_semaphore()
    pl.semaphore_signal(barrier, inc=1, device_id=(group, below), device_id_type=pl.DeviceIdType.MESH)
    pl.semaphore_wait(barrier, 1)
    rows, width = shape_ref.shape
    blocks = width // LANES
    bodies = rows // BODY_ROWS
    pairs = index_ref.shape[1]
    copies = []

    def send(source, slot):
        copy = pltpu.make_async_remote_copy(
            src_ref=source,
            dst_ref=lower.at[slot],
            send_sem=send_sem.at[slot],
            recv_sem=recv_sem.at[slot],
            device_id=(group, above),
            device_id_type=pl.DeviceIdType.MESH,
        )
        copy.start()
        copies.append(copy)

    send(shape_ref, 0)
    lane = lax.broadcasted_iota(jnp.int32, (LANES, pairs), 0)
    own_hot[...] = jnp.where(lane == index_ref[0:1, :], 1.0, 0.0).astype(jnp.bfloat16)
    far_hot[...] = jnp.where(lane == index_ref[3:4, :], 1.0, 0.0).astype(jnp.bfloat16)
    own_block, own_body = index_ref[1:2, :], index_ref[2:3, :]
    far_block, far_body = index_ref[4:5, :], index_ref[5:6, :]
    row_body = lax.broadcasted_iota(jnp.int32, (rows, pairs), 0) // BODY_ROWS
    for sweep in range(ITERS):
        shape = shape_ref[...] if sweep == 0 else current[sweep]
        own = pick(shape, own_hot[...], own_block, own_body)
        centroid = jnp.sum(shape, axis=1, keepdims=True) * (1.0 / verts)
        base = mass_weight * predicted_ref[...] + shape_weight * (centroid + rest_ref[...])
        copies[sweep].wait_recv()
        far = pick(lower[sweep], far_hot[...], far_block, far_body)
        diff = own - far
        square = jnp.sum(diff * diff, axis=0, keepdims=True) * (1.0 / bodies)
        push = contact_gain * jnp.exp(square * (-1.0 / contact_range)) * diff
        push = jnp.where(row_body == own_body, push, 0.0)
        parts = [
            jnp.concatenate(
                [jnp.where(own_block == h, part.astype(jnp.float32), 0.0) for h in range(blocks)], axis=0
            ).astype(jnp.bfloat16)
            for part in pieces(push)
        ]
        added = lax.dot_general(
            jnp.concatenate(parts, axis=0), own_hot[...], (((1,), (1,)), ((), ())),
            preferred_element_type=jnp.float32,
        )
        size = rows * blocks
        added = added[:size] + added[size : 2 * size] + added[2 * size :]
        contact = jnp.concatenate([added[h * rows : (h + 1) * rows] for h in range(blocks)], axis=1)
        rhs = base + contact
        split = jnp.concatenate([part.astype(jnp.float32) for part in pieces(rhs)], axis=0).astype(jnp.bfloat16)
        by_high = jnp.dot(split, high_ref[...], preferred_element_type=jnp.float32)
        by_middle = jnp.dot(split, middle_ref[...], preferred_element_type=jnp.float32)
        both = by_high + by_middle
        shape = both[:rows] + both[rows : 2 * rows] + both[2 * rows :]
        if sweep < ITERS - 1:
            current[sweep + 1] = shape
            send(current.at[sweep + 1], sweep + 1)
        else:
            out_ref[...] = shape
    for copy in copies:
        copy.wait_send()


def run_bodies(verts, shape, predicted, rest, high, middle, index):
    rows, width = shape.shape
    pairs = index.shape[1]
    return pl.pallas_call(
        functools.partial(bodies_kernel, lax.axis_size("brick"), verts),
        out_shape=jax.ShapeDtypeStruct((rows, width), jnp.float32),
        in_specs=[pl.BlockSpec(memory_space=pltpu.VMEM)] * 6,
        out_specs=pl.BlockSpec(memory_space=pltpu.VMEM),
        scratch_shapes=[
            pltpu.VMEM((LANES, pairs), jnp.bfloat16),
            pltpu.VMEM((LANES, pairs), jnp.bfloat16),
            pltpu.VMEM((ITERS, rows, width), jnp.float32),
            pltpu.VMEM((ITERS, rows, width), jnp.float32),
            pltpu.SemaphoreType.DMA((ITERS,)),
            pltpu.SemaphoreType.DMA((ITERS,)),
        ],
        compiler_params=pltpu.CompilerParams(collective_id=0, has_side_effects=True),
    )(shape, predicted, rest, high, middle, index)


def on_device(
    populations, positions, rest_shape, inverse, sample_cells, vertex_slots, pair_own, pair_far
):
    exact = lax.Precision.HIGHEST
    brick_count = lax.axis_size("brick")
    slot_count = sample_cells.shape[1]
    peer_count = slot_count // brick_count
    bodies, verts = positions.shape[1:]
    width = -(-verts // LANES) * LANES
    pad = width - verts
    grid_shape = populations.shape[1:]
    lanes = grid_shape[2]
    lines = grid_shape[0] * grid_shape[1]

    def to_rows(value):
        return jnp.pad(value.transpose(1, 0, 2), ((0, 0), (0, 1), (0, pad))).reshape(bodies * BODY_ROWS, width)

    def from_rows(value):
        return value.reshape(bodies, BODY_ROWS, width)[:, :3, :verts].transpose(1, 0, 2)

    request = sample_cells[0]
    cell_lane = (request[None, :] % lanes == jnp.arange(lanes)[:, None]).astype(jnp.float32)
    cell_line = (request[None, :] // lanes == jnp.arange(lines)[:, None]).astype(jnp.float32)
    slots = jnp.pad(vertex_slots.reshape(bodies, verts), ((0, 0), (0, pad)), constant_values=-1)
    slot_hot = (slots[:, None, :] == jnp.arange(slot_count)[None, :, None]).astype(jnp.float32)

    def places(index):
        body, vertex = index // verts, index % verts
        return [vertex % LANES, vertex // LANES, body]

    index = jnp.stack(places(pair_own[0]) + places(pair_far[0]) + [pair_own[0]] * 2, axis=0)
    full = jnp.pad(inverse, ((0, pad), (0, pad)))
    high = lax.reduce_precision(full, 8, 7)
    middle = (full - high).astype(jnp.bfloat16)
    high = high.astype(jnp.bfloat16)
    rest = to_rows(jnp.broadcast_to(rest_shape[:, None, :], positions.shape))
    dist = populations
    shape = to_rows(positions)
    for step_index in range(STEPS):
        density, momentum = moments(dist)
        flow = (momentum / density).reshape(3, lines, lanes)
        outgoing = jnp.einsum("cxl,lk->cxk", flow, cell_lane, precision=exact)
        outgoing = jnp.sum(outgoing * cell_line[None], axis=1)
        received = lax.all_to_all(
            outgoing.reshape(3, brick_count, peer_count), "brick", split_axis=1, concat_axis=1, tiled=True
        ).reshape(3, slot_count)
        received = jnp.pad(received, ((0, 1), (0, 0)))
        vertex_flow = jnp.einsum("cs,bsv->bcv", received, slot_hot, precision=exact)
        predicted = shape + time_step * vertex_flow.reshape(shape.shape)
        shape = run_bodies(verts, shape, predicted, rest, high, middle, index)
        vertex_force = (coupling_gain * (shape - predicted)).reshape(bodies, BODY_ROWS, width)
        slot_force = jnp.einsum("bcv,bsv->cs", vertex_force, slot_hot, precision=exact)[:3]
        back = lax.all_to_all(
            slot_force.reshape(3, brick_count, peer_count), "brick", split_axis=1, concat_axis=1, tiled=True
        ).reshape(3, slot_count)
        cell_force = jnp.einsum("cxk,lk->cxl", back[:, None, :] * cell_line[None], cell_lane, precision=exact)
        force = cell_force.reshape((3,) + grid_shape)
        dist = stream(collide(dist, force))
    return (dist, from_rows(shape))


def solution(mesh):
    placed = (
        P(None, "group", "brick", None),
        P(None, ("group", "brick"), None),
        P(),
        P(),
        P(("group", "brick"), None),
        P(("group", "brick"), None),
        P(("group", "brick"), None),
        P(("group", "brick"), None),
    )
    return jax.shard_map(
        on_device,
        mesh=mesh,
        in_specs=placed,
        out_specs=(P(None, "group", "brick", None), P(None, ("group", "brick"), None)),
        check_vma=False,
    )
```

profile of v0, /device:TPU:0, one launch (start us, length us, event | category | flops | bytes accessed | tf_op | source)
XLA Modules:
  0.0 111.9 jit_solution(5672477202009498648)
XLA Ops:
  1.3 0.9 reduce_sum.129
  2.2 1.2 %broadcast_divide_fusion.1 = (f32[3,2,8,128]{3,0,2,1:T(4,128)S(1)}, f32[3,2,8,128]{3,0,2,1:T(4,128)S(1)}) fusion(f32[2,8,128]{2,1,0:T(8,128)S(1)} %reduce_sum.129, f32[19,3,1,1]{0,1,3,2:T(4,128)} %constant.122, f32[19,2,8,128]{3,2,1,0:T(8,128)} %param.16), kind=kOutput, calls=%fused_computation.180 | convolution fusion | flops 1406976 | bytes 213220 | tf_op jit(solution)/shard_map/iq,ixyz->qxyz/dot_general | solution.py:69
  4.4 6.4 %all-to-all-start = ((f32[3,8,8]{2,0,1:T(4,128)}), f32[3,8,8]{2,0,1:T(4,128)S(1)}, u32[]{:S(2)}, u32[]{:S(2)}) async-start(f32[3,8,8]{2,0,1:T(4,128)} %copy.2405), calls=%async_computation | async-start | bytes 32768 | tf_op jit(solution)/shard_map/all_to_all | solution.py:266
  10.7 0.8 and_select_fusion
  11.8 3.3 %fusion = (bf16[768,768]{1,0:T(8,128)(2,1)}, bf16[768,768]{1,0:T(8,128)(2,1)}) fusion(f32[642,642]{1,0:T(8,128)} %param.19), kind=kLoop, calls=%fused_computation.2 | loop fusion | flops 2359296 | bytes 4007952 | tf_op jit(solution)/shard_map/convert_element_type | solution.py:256
  17.6 16.6 %shard_map.167.shape_ref = f32[8,768]{1,0:T(8,128)} custom-call(f32[8,768]{1,0:T(8,128)} %copy-done.2, f32[8,768]{1,0:T(8,128)} %add.82.predicted_ref, f32[8,768]{1,0:T(8,128)} %reshape.180.rest_ref, bf16[768,768]{1,0:T(8,128)(2,1)} %get-tuple-element.17.high_ref, bf16[768,768]{1,0:T(8,128)(2,1)} %get-tuple-element.16.middle_ref, s32[8,2048]{1,0:T(8,128)} %stack.129.index_ref), custom_call_target="tpu_custom_call" | custom-call | tf_op jit(solution)/shard_map/pallas_call | solution.py:206
  34.2 0.7 subtract_multiply_fusion.1
  35.3 8.0 %all_to_all.20 = f32[3,8,8]{2,0,1:T(4,128)S(1)} all-to-all(f32[3,8,8]{2,0,1:T(4,128)S(1)} %copy.2407), channel_id=1, replica_groups=mesh['group'=4,'brick'=8] {'brick'}, dimensions={1} | all-to-all | bytes 1536 | tf_op jit(solution)/shard_map/all_to_all | solution.py:275
  44.6 2.5 %collective-permute-start.1 = (f32[19,1,8,128]{3,0,2,1:T(8,128)S(1)}, f32[19,1,8,128]{3,0,2,1:T(8,128)S(1)}, u32[]{:S(2)}, u32[]{:S(2)}) collective-permute-start(f32[19,1,8,128]{3,0,2,1:T(8,128)S(1)} %get-tuple-element.61), channel_id=1, source_target_pairs={{8,0},{16,8},{24,16},{0,24},{9,1},{17,9},{25,17},{1,25},{10,2},{18... | collective-permute-start | bytes 233480 | tf_op jit(solution)/shard_map/ppermute | solution.py:54
  47.1 3.0 %collective-permute-done.1 = f32[19,1,8,128]{3,0,2,1:T(8,128)S(1)} collective-permute-done((f32[19,1,8,128]{3,0,2,1:T(8,128)S(1)}, f32[19,1,8,128]{3,0,2,1:T(8,128)S(1)}, u32[]{:S(2)}, u32[]{:S(2)}) %collective-permute-start.1) | collective-permute-done | bytes 77856 | tf_op jit(solution)/shard_map/ppermute | solution.py:54
  50.1 2.5 %collective-permute-done = f32[19,1,8,128]{3,0,2,1:T(8,128)S(1)} collective-permute-done((f32[19,1,8,128]{3,0,2,1:T(8,128)S(1)}, f32[19,1,8,128]{3,0,2,1:T(8,128)S(1)}, u32[]{:S(2)}, u32[]{:S(2)}) %collective-permute-start) | collective-permute-done | bytes 77856 | tf_op jit(solution)/shard_map/ppermute | solution.py:52
  53.2 1.5 %collective-permute-done.3 = f32[19,4,1,128]{3,0,2,1:T(8,128)S(1)} collective-permute-done((f32[19,4,1,128]{3,0,2,1:T(8,128)S(1)}, f32[19,4,1,128]{3,0,2,1:T(8,128)S(1)}, u32[]{:S(2)}, u32[]{:S(2)}) %collective-permute-start.3) | collective-permute-done | bytes 38944 | tf_op jit(solution)/shard_map/ppermute | solution.py:54
  54.7 3.3 %collective-permute-done.2 = f32[19,4,1,128]{3,0,2,1:T(8,128)S(1)} collective-permute-done((f32[19,4,1,128]{3,0,2,1:T(8,128)S(1)}, f32[19,4,1,128]{3,0,2,1:T(8,128)S(1)}, u32[]{:S(2)}, u32[]{:S(2)}) %collective-permute-start.2) | collective-permute-done | bytes 38944 | tf_op jit(solution)/shard_map/ppermute | solution.py:52
  61.7 8.0 %all_to_all.21 = f32[3,8,8]{2,0,1:T(4,128)S(1)} all-to-all(f32[3,8,8]{2,0,1:T(4,128)S(1)} %copy.2471), channel_id=1, replica_groups=mesh['group'=4,'brick'=8] {'brick'}, dimensions={1} | all-to-all | bytes 1536 | tf_op jit(solution)/shard_map/all_to_all | solution.py:266
  70.7 13.3 %shard_map.168 = f32[8,768]{1,0:T(8,128)} custom-call(f32[8,768]{1,0:T(8,128)} %shard_map.167.shape_ref, f32[8,768]{1,0:T(8,128)} %add.91.predicted_ref, f32[8,768]{1,0:T(8,128)} %reshape.180.rest_ref, bf16[768,768]{1,0:T(8,128)(2,1)} %get-tuple-element.17.high_ref, bf16[768,768]{1,0:T(8,128)(2,1)} %get-tuple-element.16.middle_ref, s32[8,2048]{1,0:T(8,128)} %stack.129.index_ref), custom_call_target="tpu_custom_call" | custom-call | tf_op jit(solution)/shard_map/pallas_call | solution.py:206
  84.0 0.7 subtract_multiply_fusion
  85.2 10.3 %all_to_all.22 = f32[3,8,8]{2,0,1:T(4,128)S(1)} all-to-all(f32[3,8,8]{2,0,1:T(4,128)S(1)} %copy.2473), channel_id=1, replica_groups=mesh['group'=4,'brick'=8] {'brick'}, dimensions={1} | all-to-all | bytes 1536 | tf_op jit(solution)/shard_map/all_to_all | solution.py:275
  96.6 1.1 collective-permute-start.5
  97.7 1.0 collective-permute-start.4
  98.7 0.7 reshape.191
  99.5 2.4 %collective-permute-done.5 = f32[19,1,8,128]{3,0,2,1:T(8,128)S(1)} collective-permute-done((f32[19,1,8,128]{3,0,2,1:T(8,128)S(1)}, f32[19,1,8,128]{3,0,2,1:T(8,128)S(1)}, u32[]{:S(2)}, u32[]{:S(2)}) %collective-permute-start.5) | collective-permute-done | bytes 77856 | tf_op jit(solution)/shard_map/ppermute | solution.py:54
  101.9 1.5 %collective-permute-done.4 = f32[19,1,8,128]{3,0,2,1:T(8,128)S(1)} collective-permute-done((f32[19,1,8,128]{3,0,2,1:T(8,128)S(1)}, f32[19,1,8,128]{3,0,2,1:T(8,128)S(1)}, u32[]{:S(2)}, u32[]{:S(2)}) %collective-permute-start.4) | collective-permute-done | bytes 77856 | tf_op jit(solution)/shard_map/ppermute | solution.py:52
  104.5 0.8 collective-permute-done.7
  105.3 3.5 %collective-permute-done.6 = f32[19,4,1,128]{3,0,2,1:T(8,128)S(1)} collective-permute-done((f32[19,4,1,128]{3,0,2,1:T(8,128)S(1)}, f32[19,4,1,128]{3,0,2,1:T(8,128)S(1)}, u32[]{:S(2)}, u32[]{:S(2)}) %collective-permute-start.6) | collective-permute-done | bytes 38944 | tf_op jit(solution)/shard_map/ppermute | solution.py:52
  (258 shorter events, 15.9 us)
Async XLA Ops:
  4.4 12.3 %all-to-all-start = ((f32[3,8,8]{2,0,1:T(4,128)}), f32[3,8,8]{2,0,1:T(4,128)S(1)}, u32[]{:S(2)}, u32[]{:S(2)}) async-start(f32[3,8,8]{2,0,1:T(4,128)} %copy.2405), calls=%async_computation | async-start | bytes 32768 | tf_op jit(solution)/shard_map/all_to_all | solution.py:266
  11.7 3.3 %copy-start.7 = (f32[3,2,642]{2,1,0:T(2,128)S(1)}, f32[3,2,642]{2,1,0:T(2,128)}, u32[]{:S(2)}) copy-start(f32[3,2,642]{2,1,0:T(2,128)} %param.17) | copy-start | bytes 46228
  11.7 3.4 %copy-start.9 = (s32[1,1284]{1,0:T(1,128)S(1)}, s32[1,1284]{1,0:T(1,128)}, u32[]{:S(2)}) copy-start(s32[1,1284]{1,0:T(1,128)} %param.21) | copy-start | bytes 15412
  11.7 3.5 %copy-start.8 = (f32[3,642]{1,0:T(4,128)S(1)}, f32[3,642]{1,0:T(4,128)}, u32[]{:S(2)}) copy-start(f32[3,642]{1,0:T(4,128)} %param.18) | copy-start | bytes 23116
  11.8 4.2 %copy-start.5 = (s32[1,2048]{1,0:T(1,128)S(1)}, s32[1,2048]{1,0:T(1,128)}, u32[]{:S(2)}) copy-start(s32[1,2048]{1,0:T(1,128)} %param.22) | copy-start | bytes 24580
  15.1 28.7 %copy-start.6 = (f32[19,3,1,1]{0,1,3,2:T(4,128)S(1)}, f32[19,3,1,1]{0,1,3,2:T(4,128)}, u32[]{:S(2)}) copy-start(f32[19,3,1,1]{0,1,3,2:T(4,128)} %constant.122) | copy-start | bytes 688
  15.1 29.1 %copy-start = (f32[19,2,8,128]{3,2,1,0:T(8,128)S(1)}, f32[19,2,8,128]{3,2,1,0:T(8,128)}, u32[]{:S(2)}) copy-start(f32[19,2,8,128]{3,2,1,0:T(8,128)} %param.16) | copy-start | bytes 466948
  15.1 29.1 %copy-start.11 = (f32[19]{0:T(128)S(1)}, f32[19]{0:T(128)}, u32[]{:S(2)}) copy-start(f32[19]{0:T(128)} %constant.121) | copy-start | bytes 232
  15.1 29.1 %copy-start.12 = (f32[19]{0:T(128)S(1)}, f32[19]{0:T(128)}, u32[]{:S(2)}) copy-start(f32[19]{0:T(128)} %constant.102.clone) | copy-start | bytes 232
  15.2 2.4 %copy-start.2 = (f32[8,768]{1,0:T(8,128)}, f32[8,768]{1,0:T(8,128)S(1)}, u32[]{:S(2)}) copy-start(f32[8,768]{1,0:T(8,128)S(1)} %reshape.174.shape_ref) | copy-start | bytes 73732
  17.6 16.6 %copy-start.4 = (f32[8,768]{1,0:T(8,128)S(1)}, f32[8,768]{1,0:T(8,128)}, u32[]{:S(2)}) copy-start(f32[8,768]{1,0:T(8,128)} %add.82.predicted_ref) | copy-start | bytes 73732
  44.6 5.5 %collective-permute-start.1 = (f32[19,1,8,128]{3,0,2,1:T(8,128)S(1)}, f32[19,1,8,128]{3,0,2,1:T(8,128)S(1)}, u32[]{:S(2)}, u32[]{:S(2)}) collective-permute-start(f32[19,1,8,128]{3,0,2,1:T(8,128)S(1)} %get-tuple-element.61), channel_id=1, source_target_pairs={{8,0},{16,8},{24,16},{0,24},{9,1},{17,9},{25,17},{1,25},{10,2},{18... | collective-permute-start | bytes 233480 | tf_op jit(solution)/shard_map/ppermute | solution.py:54
  47.1 5.5 %collective-permute-start = (f32[19,1,8,128]{3,0,2,1:T(8,128)S(1)}, f32[19,1,8,128]{3,0,2,1:T(8,128)S(1)}, u32[]{:S(2)}, u32[]{:S(2)}) collective-permute-start(f32[19,1,8,128]{3,0,2,1:T(8,128)S(1)} %get-tuple-element.60), channel_id=1, source_target_pairs={{0,8},{8,16},{16,24},{24,0},{1,9},{9,17},{17,25},{25,1},{2,10},{10... | collective-permute-start | bytes 233480 | tf_op jit(solution)/shard_map/ppermute | solution.py:52
  52.6 2.1 %collective-permute-start.3 = (f32[19,4,1,128]{3,0,2,1:T(8,128)S(1)}, f32[19,4,1,128]{3,0,2,1:T(8,128)S(1)}, u32[]{:S(2)}, u32[]{:S(2)}) collective-permute-start(f32[19,4,1,128]{3,0,2,1:T(8,128)S(1)} %get-tuple-element.57), channel_id=1, source_target_pairs={{1,0},{2,1},{3,2},{4,3},{5,4},{6,5},{7,6},{0,7},{9,8},{10,9},{11,1... | collective-permute-start | bytes 116744 | tf_op jit(solution)/shard_map/ppermute | solution.py:54
  52.7 5.4 %collective-permute-start.2 = (f32[19,4,1,128]{3,0,2,1:T(8,128)S(1)}, f32[19,4,1,128]{3,0,2,1:T(8,128)S(1)}, u32[]{:S(2)}, u32[]{:S(2)}) collective-permute-start(f32[19,4,1,128]{3,0,2,1:T(8,128)S(1)} %get-tuple-element.56), channel_id=1, source_target_pairs={{0,1},{1,2},{2,3},{3,4},{4,5},{5,6},{6,7},{7,0},{8,9},{9,10},{10,1... | collective-permute-start | bytes 116744 | tf_op jit(solution)/shard_map/ppermute | solution.py:52
  59.2 10.9 %copy-start.1 = (f32[8,768]{1,0:T(8,128)S(1)}, f32[8,768]{1,0:T(8,128)}, u32[]{:S(2)}) copy-start(f32[8,768]{1,0:T(8,128)} %shard_map.167.shape_ref) | copy-start | bytes 73732
  70.7 13.3 %copy-start.3 = (f32[8,768]{1,0:T(8,128)S(1)}, f32[8,768]{1,0:T(8,128)}, u32[]{:S(2)}) copy-start(f32[8,768]{1,0:T(8,128)} %add.91.predicted_ref) | copy-start | bytes 73732
  96.6 5.2 %collective-permute-start.5 = (f32[19,1,8,128]{3,0,2,1:T(8,128)S(1)}, f32[19,1,8,128]{3,0,2,1:T(8,128)S(1)}, u32[]{:S(2)}, u32[]{:S(2)}) collective-permute-start(f32[19,1,8,128]{3,0,2,1:T(8,128)S(1)} %get-tuple-element.59), channel_id=1, source_target_pairs={{8,0},{16,8},{24,16},{0,24},{9,1},{17,9},{25,17},{1,25},{10,2},{18... | collective-permute-start | bytes 233480 | tf_op jit(solution)/shard_map/ppermute | solution.py:54
  97.7 5.7 %collective-permute-start.4 = (f32[19,1,8,128]{3,0,2,1:T(8,128)S(1)}, f32[19,1,8,128]{3,0,2,1:T(8,128)S(1)}, u32[]{:S(2)}, u32[]{:S(2)}) collective-permute-start(f32[19,1,8,128]{3,0,2,1:T(8,128)S(1)} %get-tuple-element.58), channel_id=1, source_target_pairs={{0,8},{8,16},{16,24},{24,0},{1,9},{9,17},{17,25},{25,1},{2,10},{10... | collective-permute-start | bytes 233480 | tf_op jit(solution)/shard_map/ppermute | solution.py:52
  103.4 1.9 %collective-permute-start.7 = (f32[19,4,1,128]{3,0,2,1:T(8,128)S(1)}, f32[19,4,1,128]{3,0,2,1:T(8,128)S(1)}, u32[]{:S(2)}, u32[]{:S(2)}) collective-permute-start(f32[19,4,1,128]{3,0,2,1:T(8,128)S(1)} %get-tuple-element.55), channel_id=1, source_target_pairs={{1,0},{2,1},{3,2},{4,3},{5,4},{6,5},{7,6},{0,7},{9,8},{10,9},{11,1... | collective-permute-start | bytes 116744 | tf_op jit(solution)/shard_map/ppermute | solution.py:54
  103.4 5.4 %collective-permute-start.6 = (f32[19,4,1,128]{3,0,2,1:T(8,128)S(1)}, f32[19,4,1,128]{3,0,2,1:T(8,128)S(1)}, u32[]{:S(2)}, u32[]{:S(2)}) collective-permute-start(f32[19,4,1,128]{3,0,2,1:T(8,128)S(1)} %get-tuple-element.54), channel_id=1, source_target_pairs={{0,1},{1,2},{2,3},{3,4},{4,5},{5,6},{6,7},{7,0},{8,9},{9,10},{10,1... | collective-permute-start | bytes 116744 | tf_op jit(solution)/shard_map/ppermute | solution.py:52
  111.2 0.7 copy-start.10
where the time goes:
time: 113 us; the launch traced here: 112 us
  Pallas kernels  29.9 us (26%)
  blocking collectives  26.3 us (23%)
  waiting for transfers between devices  18.5 us (16%)
  starting transfers between devices  12 us (11%)
  other arithmetic  10.9 us (10%)
  local copies, waits for them, and re-layouts  7.43 us (7%)
  matrix products  4.87 us (4%)
  between operations  1.93 us (2%)
    pallas_call x2, Pallas kernels, run_bodies(): pl.pallas_call(functools.partial(bodies_kernel, lax.axis_size('brick'), v...  29.9 us
    all_to_all x2, blocking collectives, on_device(): lax.all_to_all(slot_force.reshape(3, brick_count, peer_count), 'brick', s...  18.3 us
    ppermute x4, waiting for transfers between devices, extended(): lax.ppermute(tail, axis, [(i, (i + 1) % count) for i in range(count)])  10.8 us
    all_to_all x1, blocking collectives, on_device(): lax.all_to_all(outgoing.reshape(3, brick_count, peer_count), 'brick', spl...  8.02 us
    ppermute x4, waiting for transfers between devices, extended(): lax.ppermute(head, axis, [((i + 1) % count, i) for i in range(count)])  7.73 us
    all_to_all x1, starting transfers between devices, on_device(): lax.all_to_all(outgoing.reshape(3, brick_count, peer_count), 'brick', spl...  6.35 us
    ppermute x4, starting transfers between devices, extended(): lax.ppermute(head, axis, [((i + 1) % count, i) for i in range(count)])  3.67 us
    convert_element_type x1, other arithmetic, on_device(): middle = (full - high).astype(jnp.bfloat16)  3.29 us
  transfers between devices with their start and end apart: 9, of which 8 were waited for; matrix products, arithmetic and copies ran while one was open for 6% of the time, Pallas kernels for 0%

commit v1 on v0

--- a/solution.py
+++ b/solution.py
@@ -220,13 +220,67 @@
     )(shape, predicted, rest, high, middle, index)
 
 
+def swap_kernel(count, blocks_ref, out_ref, local_sem, send_sem, recv_sem):
+    me = lax.axis_index("brick")
+    group = lax.axis_index("group")
+    barrier = pltpu.get_barrier_semaphore()
+
+    def copy_to(step):
+        peer = lax.rem(me + step, count)
+        return peer, pltpu.make_async_remote_copy(
+            src_ref=blocks_ref.at[peer],
+            dst_ref=out_ref.at[me],
+            send_sem=send_sem.at[step],
+            recv_sem=recv_sem.at[step],
+            device_id=(group, peer),
+            device_id_type=pl.DeviceIdType.MESH,
+        )
+
+    @pl.loop(1, count)
+    def _(step):
+        peer = lax.rem(me + step, count)
+        pl.semaphore_signal(barrier, inc=1, device_id=(group, peer), device_id_type=pl.DeviceIdType.MESH)
+
+    own = pltpu.make_async_copy(blocks_ref.at[me], out_ref.at[me], local_sem)
+    own.start()
+    pl.semaphore_wait(barrier, count - 1)
+
+    @pl.loop(1, count)
+    def _(step):
+        copy_to(step)[1].start()
+
+    own.wait()
+
+    @pl.loop(1, count)
+    def _(step):
+        copy_to(step)[1].wait()
+
+
+def swap(value):
+    count = lax.axis_size("brick")
+    each = value.shape[1] // count
+    blocks = value.reshape(3, count, each).transpose(1, 0, 2)
+    blocks = jnp.pad(blocks, ((0, 0), (0, 5), (0, LANES - each)))
+    blocks = pl.pallas_call(
+        functools.partial(swap_kernel, count),
+        out_shape=jax.ShapeDtypeStruct(blocks.shape, jnp.float32),
+        in_specs=[pl.BlockSpec(memory_space=pltpu.VMEM)],
+        out_specs=pl.BlockSpec(memory_space=pltpu.VMEM),
+        scratch_shapes=[
+            pltpu.SemaphoreType.DMA,
+            pltpu.SemaphoreType.DMA((count,)),
+            pltpu.SemaphoreType.DMA((count,)),
+        ],
+        compiler_params=pltpu.CompilerParams(collective_id=1, has_side_effects=True),
+    )(blocks)
+    return blocks[:, :3, :each].transpose(1, 0, 2).reshape(value.shape)
+
+
 def on_device(
     populations, positions, rest_shape, inverse, sample_cells, vertex_slots, pair_own, pair_far
 ):
     exact = lax.Precision.HIGHEST
-    brick_count = lax.axis_size("brick")
     slot_count = sample_cells.shape[1]
-    peer_count = slot_count // brick_count
     bodies, verts = positions.shape[1:]
     width = -(-verts // LANES) * LANES
     pad = width - verts
@@ -263,18 +317,14 @@
         flow = (momentum / density).reshape(3, lines, lanes)
         outgoing = jnp.einsum("cxl,lk->cxk", flow, cell_lane, precision=exact)
         outgoing = jnp.sum(outgoing * cell_line[None], axis=1)
-        received = lax.all_to_all(
-            outgoing.reshape(3, brick_count, peer_count), "brick", split_axis=1, concat_axis=1, tiled=True
-        ).reshape(3, slot_count)
+        received = swap(outgoing)
         received = jnp.pad(received, ((0, 1), (0, 0)))
         vertex_flow = jnp.einsum("cs,bsv->bcv", received, slot_hot, precision=exact)
         predicted = shape + time_step * vertex_flow.reshape(shape.shape)
         shape = run_bodies(verts, shape, predicted, rest, high, middle, index)
         vertex_force = (coupling_gain * (shape - predicted)).reshape(bodies, BODY_ROWS, width)
         slot_force = jnp.einsum("bcv,bsv->cs", vertex_force, slot_hot, precision=exact)[:3]
-        back = lax.all_to_all(
-            slot_force.reshape(3, brick_count, peer_count), "brick", split_axis=1, concat_axis=1, tiled=True
-        ).reshape(3, slot_count)
+        back = swap(slot_force)
         cell_force = jnp.einsum("cxk,lk->cxl", back[:, None, :] * cell_line[None], cell_lane, precision=exact)
         force = cell_force.reshape((3,) + grid_shape)
         dist = stream(collide(dist, force))

time: 113 us -> 119 us (1.053)
  Pallas kernels: 29.9 us -> 61.4 us
  blocking collectives: 26.3 us -> 0 us
  starting transfers between devices: 12 us -> 5.69 us
  local copies, waits for them, and re-layouts: 7.43 us -> 13.1 us
    pallas_call x0 -> x4, Pallas kernels: none -> 31.7 us  [swap(): pl.pallas_call(functools.partial(swap_kernel, count), out_shape=jax.Shape...]
    all_to_all x3 -> x0, blocking collectives: 26.3 us -> none  [the longest x2 18.3 us: on_device(): lax.all_to_all(slot_force.reshape(3, brick_count, peer_count), 'brick', s...]
    all_to_all x1 -> x0, starting transfers between devices: 6.35 us -> none  [on_device(): lax.all_to_all(outgoing.reshape(3, brick_count, peer_count), 'brick', spl...]
    transpose x0 -> x8, local copies, waits for them, and re-layouts: none -> 3.07 us  [swap(): return blocks[:, :3, :each].transpose(1, 0, 2).reshape(value.shape)]
    pad x0 -> x4, local copies, waits for them, and re-layouts: none -> 2.53 us  [swap(): blocks = jnp.pad(blocks, ((0, 0), (0, 5), (0, LANES - each)))]
  transfers between devices with their start and end apart: 9 -> 8, of which waited for: 8 -> 8; matrix products, arithmetic and copies ran while one was open for 6% -> 1% of each run, Pallas kernels for 0% -> 0%
where the time goes in v1:
time: 119 us; the launch traced here: 118 us
  Pallas kernels  61.4 us (52%)
  waiting for transfers between devices  19.6 us (16%)
  local copies, waits for them, and re-layouts  13.1 us (11%)
  other arithmetic  11 us (9%)
  starting transfers between devices  5.69 us (5%)
  matrix products  4.88 us (4%)
  between operations  1.93 us (2%)
    pallas_call x4, Pallas kernels, swap(): pl.pallas_call(functools.partial(swap_kernel, count), out_shape=jax.Shape...  31.7 us
    pallas_call x2, Pallas kernels, run_bodies(): pl.pallas_call(functools.partial(bodies_kernel, lax.axis_size('brick'), v...  29.7 us
    ppermute x4, waiting for transfers between devices, extended(): lax.ppermute(tail, axis, [(i, (i + 1) % count) for i in range(count)])  11.4 us
    ppermute x4, waiting for transfers between devices, extended(): lax.ppermute(head, axis, [((i + 1) % count, i) for i in range(count)])  8.23 us
    ppermute x4, starting transfers between devices, extended(): lax.ppermute(head, axis, [((i + 1) % count, i) for i in range(count)])  4.01 us
    convert_element_type x1, other arithmetic, on_device(): middle = (full - high).astype(jnp.bfloat16)  3.32 us
    transpose x8, local copies, waits for them, and re-layouts, swap(): return blocks[:, :3, :each].transpose(1, 0, 2).reshape(value.shape)  3.07 us
    pad x4, local copies, waits for them, and re-layouts, swap(): blocks = jnp.pad(blocks, ((0, 0), (0, 5), (0, LANES - each)))  2.53 us
  transfers between devices with their start and end apart: 8, of which 8 were waited for; matrix products, arithmetic and copies ran while one was open for 1% of the time, Pallas kernels for 0%

profile of v1, /device:TPU:0, one launch (start us, length us, event | category | flops | bytes accessed | tf_op | source)
XLA Modules:
  0.0 117.6 jit_solution(2602184994400222049)
XLA Ops:
  2.9 0.9 reduce_sum.129
  3.8 1.2 %broadcast_divide_fusion.1 = (f32[3,2,8,128]{3,0,2,1:T(4,128)S(1)}, f32[3,2,8,128]{3,0,2,1:T(4,128)S(1)}) fusion(f32[2,8,128]{2,1,0:T(8,128)S(1)} %reduce_sum.129, f32[19,3,1,1]{0,1,3,2:T(4,128)} %constant.130, f32[19,2,8,128]{3,2,1,0:T(8,128)} %param.16), kind=kOutput, calls=%fused_computation.188 | convolution fusion | flops 1406976 | bytes 213220 | tf_op jit(solution)/shard_map/iq,ixyz->qxyz/dot_general | solution.py:69
  6.0 8.8 %shard_map.167 = f32[8,8,128]{2,1,0:T(8,128)} custom-call(f32[8,8,128]{2,1,0:T(8,128)} %pad.39.blocks_ref), custom_call_target="tpu_custom_call" | custom-call | tf_op jit(solution)/shard_map/pallas_call | solution.py:264
  14.8 0.8 slice_bitcast_fusion.4
  17.2 3.3 %fusion = (bf16[768,768]{1,0:T(8,128)(2,1)}, bf16[768,768]{1,0:T(8,128)(2,1)}) fusion(f32[642,642]{1,0:T(8,128)} %param.19), kind=kLoop, calls=%fused_computation.2 | loop fusion | flops 2359296 | bytes 4007952 | tf_op jit(solution)/shard_map/convert_element_type | solution.py:310
  22.2 16.1 %shard_map.168.shape_ref = f32[8,768]{1,0:T(8,128)} custom-call(f32[8,768]{1,0:T(8,128)} %copy-done.2, f32[8,768]{1,0:T(8,128)} %add.90.predicted_ref, f32[8,768]{1,0:T(8,128)} %reshape.180.rest_ref, bf16[768,768]{1,0:T(8,128)(2,1)} %get-tuple-element.15.high_ref, bf16[768,768]{1,0:T(8,128)(2,1)} %get-tuple-element.14.middle_ref, s32[8,2048]{1,0:T(8,128)} %stack.129.index_ref), custom_call_target="tpu_custom_call" | custom-call | tf_op jit(solution)/shard_map/pallas_call | solution.py:206
  40.1 7.2 %shard_map.169 = f32[8,8,128]{2,1,0:T(8,128)} custom-call(f32[8,8,128]{2,1,0:T(8,128)} %pad.44.blocks_ref), custom_call_target="tpu_custom_call" | custom-call | tf_op jit(solution)/shard_map/pallas_call | solution.py:264
  47.4 0.8 slice_bitcast_fusion.3
  49.4 2.5 %collective-permute-start.1 = (f32[19,1,8,128]{3,0,2,1:T(8,128)S(1)}, f32[19,1,8,128]{3,0,2,1:T(8,128)S(1)}, u32[]{:S(2)}, u32[]{:S(2)}) collective-permute-start(f32[19,1,8,128]{3,0,2,1:T(8,128)S(1)} %get-tuple-element.59), channel_id=1, source_target_pairs={{8,0},{16,8},{24,16},{0,24},{9,1},{17,9},{25,17},{1,25},{10,2},{18... | collective-permute-start | bytes 233480 | tf_op jit(solution)/shard_map/ppermute | solution.py:54
  51.9 3.2 %collective-permute-done.1 = f32[19,1,8,128]{3,0,2,1:T(8,128)S(1)} collective-permute-done((f32[19,1,8,128]{3,0,2,1:T(8,128)S(1)}, f32[19,1,8,128]{3,0,2,1:T(8,128)S(1)}, u32[]{:S(2)}, u32[]{:S(2)}) %collective-permute-start.1) | collective-permute-done | bytes 77856 | tf_op jit(solution)/shard_map/ppermute | solution.py:54
  55.1 2.3 %collective-permute-done = f32[19,1,8,128]{3,0,2,1:T(8,128)S(1)} collective-permute-done((f32[19,1,8,128]{3,0,2,1:T(8,128)S(1)}, f32[19,1,8,128]{3,0,2,1:T(8,128)S(1)}, u32[]{:S(2)}, u32[]{:S(2)}) %collective-permute-start) | collective-permute-done | bytes 77856 | tf_op jit(solution)/shard_map/ppermute | solution.py:52
  58.0 1.3 %collective-permute-done.3 = f32[19,4,1,128]{3,0,2,1:T(8,128)S(1)} collective-permute-done((f32[19,4,1,128]{3,0,2,1:T(8,128)S(1)}, f32[19,4,1,128]{3,0,2,1:T(8,128)S(1)}, u32[]{:S(2)}, u32[]{:S(2)}) %collective-permute-start.3) | collective-permute-done | bytes 38944 | tf_op jit(solution)/shard_map/ppermute | solution.py:54
  59.3 3.7 %collective-permute-done.2 = f32[19,4,1,128]{3,0,2,1:T(8,128)S(1)} collective-permute-done((f32[19,4,1,128]{3,0,2,1:T(8,128)S(1)}, f32[19,4,1,128]{3,0,2,1:T(8,128)S(1)}, u32[]{:S(2)}, u32[]{:S(2)}) %collective-permute-start.2) | collective-permute-done | bytes 38944 | tf_op jit(solution)/shard_map/ppermute | solution.py:52
  67.4 6.9 %shard_map.170 = f32[8,8,128]{2,1,0:T(8,128)} custom-call(f32[8,8,128]{2,1,0:T(8,128)} %pad.45.blocks_ref), custom_call_target="tpu_custom_call" | custom-call | tf_op jit(solution)/shard_map/pallas_call | solution.py:264
  74.3 0.8 slice_bitcast_fusion.2
  76.0 13.6 %shard_map.171 = f32[8,768]{1,0:T(8,128)} custom-call(f32[8,768]{1,0:T(8,128)} %shard_map.168.shape_ref, f32[8,768]{1,0:T(8,128)} %add.99.predicted_ref, f32[8,768]{1,0:T(8,128)} %reshape.180.rest_ref, bf16[768,768]{1,0:T(8,128)(2,1)} %get-tuple-element.15.high_ref, bf16[768,768]{1,0:T(8,128)(2,1)} %get-tuple-element.14.middle_ref, s32[8,2048]{1,0:T(8,128)} %stack.129.index_ref), custom_call_target="tpu_custom_call" | custom-call | tf_op jit(solution)/shard_map/pallas_call | solution.py:206
  89.6 0.8 subtract_multiply_fusion
  91.5 8.7 %shard_map.172 = f32[8,8,128]{2,1,0:T(8,128)} custom-call(f32[8,8,128]{2,1,0:T(8,128)} %pad.47.blocks_ref), custom_call_target="tpu_custom_call" | custom-call | tf_op jit(solution)/shard_map/pallas_call | solution.py:264
  100.2 0.8 slice_bitcast_fusion.1
  102.2 1.4 %collective-permute-start.5 = (f32[19,1,8,128]{3,0,2,1:T(8,128)S(1)}, f32[19,1,8,128]{3,0,2,1:T(8,128)S(1)}, u32[]{:S(2)}, u32[]{:S(2)}) collective-permute-start(f32[19,1,8,128]{3,0,2,1:T(8,128)S(1)} %get-tuple-element.57), channel_id=1, source_target_pairs={{8,0},{16,8},{24,16},{0,24},{9,1},{17,9},{25,17},{1,25},{10,2},{18... | collective-permute-start | bytes 233480 | tf_op jit(solution)/shard_map/ppermute | solution.py:54
  104.3 2.9 %collective-permute-done.5 = f32[19,1,8,128]{3,0,2,1:T(8,128)S(1)} collective-permute-done((f32[19,1,8,128]{3,0,2,1:T(8,128)S(1)}, f32[19,1,8,128]{3,0,2,1:T(8,128)S(1)}, u32[]{:S(2)}, u32[]{:S(2)}) %collective-permute-start.5) | collective-permute-done | bytes 77856 | tf_op jit(solution)/shard_map/ppermute | solution.py:54
  107.1 2.0 %collective-permute-done.4 = f32[19,1,8,128]{3,0,2,1:T(8,128)S(1)} collective-permute-done((f32[19,1,8,128]{3,0,2,1:T(8,128)S(1)}, f32[19,1,8,128]{3,0,2,1:T(8,128)S(1)}, u32[]{:S(2)}, u32[]{:S(2)}) %collective-permute-start.4) | collective-permute-done | bytes 77856 | tf_op jit(solution)/shard_map/ppermute | solution.py:52
  110.3 0.9 collective-permute-done.7
  111.2 3.4 %collective-permute-done.6 = f32[19,4,1,128]{3,0,2,1:T(8,128)S(1)} collective-permute-done((f32[19,4,1,128]{3,0,2,1:T(8,128)S(1)}, f32[19,4,1,128]{3,0,2,1:T(8,128)S(1)}, u32[]{:S(2)}, u32[]{:S(2)}) %collective-permute-start.6) | collective-permute-done | bytes 38944 | tf_op jit(solution)/shard_map/ppermute | solution.py:52
  (263 shorter events, 21.5 us)
Async XLA Ops:
  2.1 18.8 %copy-start.2 = (f32[8,768]{1,0:T(8,128)}, f32[8,768]{1,0:T(8,128)S(1)}, u32[]{:S(2)}) copy-start(f32[8,768]{1,0:T(8,128)S(1)} %reshape.174.shape_ref) | copy-start | bytes 73732
  17.2 3.3 %copy-start.6 = (s32[1,2048]{1,0:T(1,128)S(1)}, s32[1,2048]{1,0:T(1,128)}, u32[]{:S(2)}) copy-start(s32[1,2048]{1,0:T(1,128)} %param.22) | copy-start | bytes 24580
  17.2 3.3 %copy-start.8 = (s32[1,2048]{1,0:T(1,128)S(1)}, s32[1,2048]{1,0:T(1,128)}, u32[]{:S(2)}) copy-start(s32[1,2048]{1,0:T(1,128)} %param.23) | copy-start | bytes 24580
  20.6 28.0 %copy-start.7 = (f32[19,3,1,1]{0,1,3,2:T(4,128)S(1)}, f32[19,3,1,1]{0,1,3,2:T(4,128)}, u32[]{:S(2)}) copy-start(f32[19,3,1,1]{0,1,3,2:T(4,128)} %constant.130) | copy-start | bytes 688
  20.6 28.4 %copy-start = (f32[19,2,8,128]{3,2,1,0:T(8,128)S(1)}, f32[19,2,8,128]{3,2,1,0:T(8,128)}, u32[]{:S(2)}) copy-start(f32[19,2,8,128]{3,2,1,0:T(8,128)} %param.16) | copy-start | bytes 466948
  20.6 28.4 %copy-start.10 = (f32[19]{0:T(128)S(1)}, f32[19]{0:T(128)}, u32[]{:S(2)}) copy-start(f32[19]{0:T(128)} %constant.129) | copy-start | bytes 232
  20.6 28.4 %copy-start.11 = (f32[19]{0:T(128)S(1)}, f32[19]{0:T(128)}, u32[]{:S(2)}) copy-start(f32[19]{0:T(128)} %constant.102.clone) | copy-start | bytes 232
  21.5 16.9 %copy-start.4 = (f32[8,768]{1,0:T(8,128)S(1)}, f32[8,768]{1,0:T(8,128)}, u32[]{:S(2)}) copy-start(f32[8,768]{1,0:T(8,128)} %add.90.predicted_ref) | copy-start | bytes 73732
  49.4 5.7 %collective-permute-start.1 = (f32[19,1,8,128]{3,0,2,1:T(8,128)S(1)}, f32[19,1,8,128]{3,0,2,1:T(8,128)S(1)}, u32[]{:S(2)}, u32[]{:S(2)}) collective-permute-start(f32[19,1,8,128]{3,0,2,1:T(8,128)S(1)} %get-tuple-element.59), channel_id=1, source_target_pairs={{8,0},{16,8},{24,16},{0,24},{9,1},{17,9},{25,17},{1,25},{10,2},{18... | collective-permute-start | bytes 233480 | tf_op jit(solution)/shard_map/ppermute | solution.py:54
  51.9 5.5 %collective-permute-start = (f32[19,1,8,128]{3,0,2,1:T(8,128)S(1)}, f32[19,1,8,128]{3,0,2,1:T(8,128)S(1)}, u32[]{:S(2)}, u32[]{:S(2)}) collective-permute-start(f32[19,1,8,128]{3,0,2,1:T(8,128)S(1)} %get-tuple-element.58), channel_id=1, source_target_pairs={{0,8},{8,16},{16,24},{24,0},{1,9},{9,17},{17,25},{25,1},{2,10},{10... | collective-permute-start | bytes 233480 | tf_op jit(solution)/shard_map/ppermute | solution.py:52
  57.4 1.9 %collective-permute-start.3 = (f32[19,4,1,128]{3,0,2,1:T(8,128)S(1)}, f32[19,4,1,128]{3,0,2,1:T(8,128)S(1)}, u32[]{:S(2)}, u32[]{:S(2)}) collective-permute-start(f32[19,4,1,128]{3,0,2,1:T(8,128)S(1)} %get-tuple-element.55), channel_id=1, source_target_pairs={{1,0},{2,1},{3,2},{4,3},{5,4},{6,5},{7,6},{0,7},{9,8},{10,9},{11,1... | collective-permute-start | bytes 116744 | tf_op jit(solution)/shard_map/ppermute | solution.py:54
  57.5 5.5 %collective-permute-start.2 = (f32[19,4,1,128]{3,0,2,1:T(8,128)S(1)}, f32[19,4,1,128]{3,0,2,1:T(8,128)S(1)}, u32[]{:S(2)}, u32[]{:S(2)}) collective-permute-start(f32[19,4,1,128]{3,0,2,1:T(8,128)S(1)} %get-tuple-element.54), channel_id=1, source_target_pairs={{0,1},{1,2},{2,3},{3,4},{4,5},{5,6},{6,7},{7,0},{8,9},{9,10},{10,1... | collective-permute-start | bytes 116744 | tf_op jit(solution)/shard_map/ppermute | solution.py:52
  64.3 11.1 %copy-start.1 = (f32[8,768]{1,0:T(8,128)S(1)}, f32[8,768]{1,0:T(8,128)}, u32[]{:S(2)}) copy-start(f32[8,768]{1,0:T(8,128)} %shard_map.168.shape_ref) | copy-start | bytes 73732
  76.0 13.6 %copy-start.5 = (f32[8,768]{1,0:T(8,128)S(1)}, f32[8,768]{1,0:T(8,128)}, u32[]{:S(2)}) copy-start(f32[8,768]{1,0:T(8,128)} %add.99.predicted_ref) | copy-start | bytes 73732
  89.6 14.6 %copy-start.3 = (f32[8,768]{1,0:T(8,128)S(1)}, f32[8,768]{1,0:T(8,128)}, u32[]{:S(2)}) copy-start(f32[8,768]{1,0:T(8,128)} %shard_map.171) | copy-start | bytes 73732
  102.2 4.9 %collective-permute-start.5 = (f32[19,1,8,128]{3,0,2,1:T(8,128)S(1)}, f32[19,1,8,128]{3,0,2,1:T(8,128)S(1)}, u32[]{:S(2)}, u32[]{:S(2)}) collective-permute-start(f32[19,1,8,128]{3,0,2,1:T(8,128)S(1)} %get-tuple-element.57), channel_id=1, source_target_pairs={{8,0},{16,8},{24,16},{0,24},{9,1},{17,9},{25,17},{1,25},{10,2},{18... | collective-permute-start | bytes 233480 | tf_op jit(solution)/shard_map/ppermute | solution.py:54
  103.6 5.5 %collective-permute-start.4 = (f32[19,1,8,128]{3,0,2,1:T(8,128)S(1)}, f32[19,1,8,128]{3,0,2,1:T(8,128)S(1)}, u32[]{:S(2)}, u32[]{:S(2)}) collective-permute-start(f32[19,1,8,128]{3,0,2,1:T(8,128)S(1)} %get-tuple-element.56), channel_id=1, source_target_pairs={{0,8},{8,16},{16,24},{24,0},{1,9},{9,17},{17,25},{25,1},{2,10},{10... | collective-permute-start | bytes 233480 | tf_op jit(solution)/shard_map/ppermute | solution.py:52
  109.1 2.1 %collective-permute-start.7 = (f32[19,4,1,128]{3,0,2,1:T(8,128)S(1)}, f32[19,4,1,128]{3,0,2,1:T(8,128)S(1)}, u32[]{:S(2)}, u32[]{:S(2)}) collective-permute-start(f32[19,4,1,128]{3,0,2,1:T(8,128)S(1)} %get-tuple-element.53), channel_id=1, source_target_pairs={{1,0},{2,1},{3,2},{4,3},{5,4},{6,5},{7,6},{0,7},{9,8},{10,9},{11,1... | collective-permute-start | bytes 116744 | tf_op jit(solution)/shard_map/ppermute | solution.py:54
  109.2 5.4 %collective-permute-start.6 = (f32[19,4,1,128]{3,0,2,1:T(8,128)S(1)}, f32[19,4,1,128]{3,0,2,1:T(8,128)S(1)}, u32[]{:S(2)}, u32[]{:S(2)}) collective-permute-start(f32[19,4,1,128]{3,0,2,1:T(8,128)S(1)} %get-tuple-element.52), channel_id=1, source_target_pairs={{0,1},{1,2},{2,3},{3,4},{4,5},{5,6},{6,7},{7,0},{8,9},{9,10},{10,1... | collective-permute-start | bytes 116744 | tf_op jit(solution)/shard_map/ppermute | solution.py:52
  117.0 0.7 copy-start.9
